TPU v7x, 32 devices: a whole 2x2x4 slice. The times are simulated.
32 devices in a mesh: group: 4 (over z), dom: 8 (over y, x, core).
Axes of the slice: x: 2, y: 2, z: 4, core: 2. Of those that a mesh axis runs over, the one named last changes fastest.
Arguments:
- hot_rows: bfloat16 [4096, 1024], P(('group', 'dom')), may hold values from -6 to 6
- cold_codes: bfloat16 [4096, 1024], P(('group', 'dom')), may hold values from -127 to 127
- scale_index: int32 [4096], P(('group', 'dom')), may hold values from 0 to 255
- scale_table: float32 [256], replicated, may hold values from 0.004 to 0.04
- stale_rows: bfloat16 [4096, 1024], P(('group', 'dom')), may hold values from -6 to 6
- tile_index: int32 [64, 3], P(('group', 'dom')), may hold values from 0 to 2
- tile_count: int32 [64], P(('group', 'dom')), may hold values from 1 to 3
- tile_values: bfloat16 [64, 3, 128, 128], P(('group', 'dom')), may hold values from -0.3125 to 0.3125
- weight: bfloat16 [1024, 1024], P('dom'), may hold values from -0.1875 to 0.1875
- out_grad: bfloat16 [8192, 1024], P(('group', 'dom')), may hold values from -6 to 6
- stale_grads: bfloat16 [4096, 1024], P(('group', 'dom')), may hold values from -6 to 6
- send_rows: int32 [256, 16], P(('group', 'dom')), may hold values from 0 to 255
Outputs:
- activations: bfloat16 [8192, 1024], P(('group', 'dom'))
- feature_grad: bfloat16 [8192, 1024], P(('group', 'dom'))
- weight_grad: float32 [1024, 1024], P('dom')
- next_rows: bfloat16 [4096, 1024], P(('group', 'dom'))
- next_grads: bfloat16 [4096, 1024], P(('group', 'dom'))
Inputs may be any that keep to these rules, and one draw needn't show every extreme that they name: `send_rows`: rows may repeat.
All inputs are finite; a program needn't handle non-finite values.
Results may differ from a plain program's by a relative error of at most 0.0061.
Values may be sent and summed in bfloat16 or wider, within the bound.
A program may use at most 64 MiB of HBM per device.

v0:
```python
import jax
import jax.numpy as jnp
from jax import lax
from jax.sharding import PartitionSpec as P


def dequantize(cold_codes, scale_index, scale_table):
    levels = jnp.arange(scale_table.shape[0], dtype=jnp.int32)
    lookup = jnp.sum(
        jnp.where(
            scale_index[:, None] == levels[None, :],
            scale_table[None, :],
            jnp.zeros_like(scale_table)[None, :],
        ),
        axis=1,
    )
    return (cold_codes.astype(jnp.float32) * lookup[:, None]).astype(jnp.bfloat16)


def silu_parts(preact):
    logistic = jax.nn.sigmoid(preact)
    return (preact * logistic, logistic * (1.0 + preact * (1.0 - logistic)))


def local(
    hot_rows,
    cold_codes,
    scale_index,
    scale_table,
    stale_rows,
    tile_index,
    tile_count,
    tile_values,
    weight,
    out_grad,
    stale_grads,
    send_rows,
):
    tile_slots = tile_values.shape[1]
    cluster_rows = tile_values.shape[2]
    local_rows = jnp.concatenate(
        [hot_rows, dequantize(cold_codes, scale_index, scale_table)], axis=0
    )
    row_count = local_rows.shape[0]
    sends = send_rows.reshape(-1)
    outgoing = jnp.take(local_rows, sends, axis=0)
    next_rows = lax.all_to_all(outgoing, "dom", split_axis=0, concat_axis=0, tiled=True)
    source = jnp.concatenate([local_rows, stale_rows], axis=0)
    src_count = source.shape[0] // cluster_rows
    live_mask = jnp.arange(tile_slots, dtype=jnp.int32)[None, :] < tile_count[:, None]
    masked = jnp.where(
        live_mask[:, :, None, None], tile_values, jnp.zeros_like(tile_values)
    ).astype(jnp.float32)
    selector = (
        tile_index[:, :, None] == jnp.arange(src_count, dtype=jnp.int32)[None, None, :]
    ).astype(jnp.float32)
    operator = jnp.einsum("ckj,ckab->cajb", selector, masked, precision=lax.Precision.HIGHEST)
    operator = operator.reshape(row_count, src_count * cluster_rows)
    hidden = jnp.dot(operator, source.astype(jnp.float32), precision=lax.Precision.HIGHEST)
    hidden = hidden.astype(jnp.bfloat16)
    preact = jnp.dot(
        hidden,
        lax.all_gather(weight, "dom", axis=0, tiled=True),
        preferred_element_type=jnp.float32,
    )
    activ, slope = silu_parts(preact)
    activations = activ.astype(jnp.bfloat16)
    pre_grad = (out_grad.astype(jnp.float32) * slope).astype(jnp.bfloat16)
    hid_grad = lax.dot_general(
        pre_grad,
        lax.all_gather(weight, "dom", axis=0, tiled=True),
        (((1,), (1,)), ((), ())),
        preferred_element_type=jnp.float32,
    )
    hid_grad = hid_grad.astype(jnp.bfloat16)
    partial_value = lax.dot_general(
        hidden, pre_grad, (((0,), (0,)), ((), ())), preferred_element_type=jnp.float32
    )
    block_sum = lax.psum_scatter(partial_value, "dom", scatter_dimension=0, tiled=True)
    weight_grad = lax.psum(block_sum, "group")
    src_grad = lax.dot_general(
        operator,
        hid_grad.astype(jnp.float32),
        (((0,), (0,)), ((), ())),
        precision=lax.Precision.HIGHEST,
    )
    bound_grad = src_grad[row_count:].astype(jnp.bfloat16)
    next_grads = lax.all_to_all(bound_grad, "dom", split_axis=0, concat_axis=0, tiled=True)
    placing = (jnp.arange(row_count, dtype=jnp.int32)[:, None] == sends[None, :]).astype(
        jnp.bfloat16
    )
    returned = jnp.dot(placing, stale_grads, preferred_element_type=jnp.float32)
    feature_grad = (src_grad[:row_count] + returned).astype(jnp.bfloat16)
    return (activations, feature_grad, weight_grad, next_rows, next_grads)


def solution(mesh):
    placed = (
        P(("group", "dom"), None),
        P(("group", "dom"), None),
        P(("group", "dom")),
        P(),
        P(("group", "dom"), None),
        P(("group", "dom"), None),
        P(("group", "dom")),
        P(("group", "dom"), None, None, None),
        P("dom", None),
        P(("group", "dom"), None),
        P(("group", "dom"), None),
        P(("group", "dom"), None),
    )
    return jax.shard_map(
        local,
        mesh=mesh,
        in_specs=placed,
        out_specs=(
            P(("group", "dom"), None),
            P(("group", "dom"), None),
            P("dom", None),
            P(("group", "dom"), None),
            P(("group", "dom"), None),
        ),
        check_vma=False,
    )
```

profile of v0, /device:TPU:0, one launch (start us, length us, event | category | flops | bytes accessed | tf_op | source)
XLA Modules:
  0.0 148.6 jit_solution(3321438472732656839)
XLA Ops:
  7.2 0.0 all-gather.2.cloned.1.call-start
  7.2 0.7 all-gather.2.cloned.1.call-update
  7.9 0.0 reduce-scatter.2.cloned.1.call-start
  8.0 0.9 select_reduce_fusion
  8.8 0.7 iota_compare_fusion.4
  9.6 1.0 broadcast_select_fusion.1
  10.6 1.1 multiply_convert_fusion.2
  11.6 1.0 fusion.11
  12.6 2.0 %convolution_convert_fusion = bf16[256,1024]{1,0:T(8,128)(2,1)S(1)} fusion(bf16[128,1024]{1,0:T(8,128)(2,1)} %param.16, bf16[128,1024]{1,0:T(8,128)(2,1)S(1)} %multiply_convert_fusion.2, bf16[128,1024]{1,0:T(8,128)(2,1)} %param.12, f32[32,8,3,128]{3,2,1,0:T(4,128)S(1)} %bitcast.25), kind=kOutput, calls=%fused_computation.2 | convolution fusion | flops 1210580992 | bytes 1703936 | tf_op jit(solution)/shard_map/dot_general | solution.py:59
  14.6 25.8 %all-gather.2.cloned.1.call-done = bf16[1024,1024]{1,0:T(8,128)(2,1)} async-done(((bf16[128,1024]{1,0:T(8,128)(2,1)}), bf16[1024,1024]{1,0:T(8,128)(2,1)}) %all-gather.2.cloned.1.call-update) | async-done | bytes 2097168 | tf_op jit(solution)/shard_map/all_gather | solution.py:63
  40.4 3.2 %multiply_convert_fusion.1 = (bf16[256,1024]{1,0:T(8,128)(2,1)}, f32[256,1024]{1,0:T(8,128)S(1)}) fusion(bf16[256,1024]{1,0:T(8,128)(2,1)S(1)} %convolution_convert_fusion, bf16[1024,1024]{1,0:T(8,128)(2,1)} %all-gather.2.cloned.1.call-done), kind=kOutput, calls=%fused_computation.6 | convolution fusion | flops 538181632 | bytes 4194304 | tf_op jit(solution)/shard_map/dot_general | solution.py:61
  43.6 2.9 %fusion.19 = f32[1024,1024]{1,0:T(8,128)} fusion(bf16[256,1024]{1,0:T(8,128)(2,1)S(1)} %convolution_convert_fusion, f32[256,1024]{1,0:T(8,128)S(1)} %get-tuple-element.6, bf16[256,1024]{1,0:T(8,128)(2,1)S(1)} %copy-done.1), kind=kOutput, calls=%fused_computation.39 | convolution fusion | flops 539492352 | bytes 6291456 | tf_op jit(solution)/shard_map/dot_general | solution.py:76
  46.5 0.7 copy-done.3
  47.1 0.1 reshape.86
  47.2 0.2 copy-done.2
  47.5 0.9 gather_fusion
  48.3 0.8 broadcast_select_fusion
  49.1 3.4 %all-to-all-start = ((bf16[8,16,1024]{2,1,0:T(8,128)(2,1)}), bf16[8,16,1024]{2,1,0:T(8,128)(2,1)S(1)}, u32[]{:S(2)}, u32[]{:S(2)}) async-start(bf16[8,16,1024]{2,1,0:T(8,128)(2,1)} %broadcast_select_fusion), calls=%async_computation.1 | async-start | bytes 524288 | tf_op jit(solution)/shard_map/all_to_all | solution.py:47
  52.5 0.0 all-reduce.2.cloned.1.call-start
  52.6 0.1 eq.48
  52.7 6.7 %all-to-all-done = bf16[8,16,1024]{2,1,0:T(8,128)(2,1)S(1)} async-done(((bf16[8,16,1024]{2,1,0:T(8,128)(2,1)}), bf16[8,16,1024]{2,1,0:T(8,128)(2,1)S(1)}, u32[]{:S(2)}, u32[]{:S(2)}) %all-to-all-start) | async-done | bytes 262176 | tf_op jit(solution)/shard_map/all_to_all | solution.py:47
  59.4 3.3 %convolution_convert_fusion.1 = bf16[256,1024]{1,0:T(8,128)(2,1)} fusion(bf16[1024,1024]{1,0:T(8,128)(2,1)} %all-gather.2.cloned.1.call-done, f32[256,1024]{1,0:T(8,128)S(1)} %get-tuple-element.6, bf16[256,1024]{1,0:T(8,128)(2,1)S(1)} %copy-done.1), kind=kOutput, calls=%fused_computation.4 | convolution fusion | flops 539754496 | bytes 4194304 | tf_op jit(solution)/shard_map/dot_general | solution.py:69
  62.7 35.0 %reduce-scatter.2.cloned.1.call-done = f32[128,1024]{1,0:T(8,128)} async-done(((f32[1024,1024]{1,0:T(8,128)}), f32[128,1024]{1,0:T(8,128)}) %reduce-scatter.2.cloned.1.call-update) | async-done | bytes 524304 | tf_op jit(solution)/shard_map/reduce_scatter | solution.py:79
  97.8 1.9 %fusion.7 = f32[384,1024]{1,0:T(8,128)S(1)} fusion(bf16[256,1024]{1,0:T(8,128)(2,1)} %convolution_convert_fusion.1, f32[32,8,3,128]{3,2,1,0:T(4,128)S(1)} %bitcast.26), kind=kOutput, calls=%fused_computation.17 | convolution fusion | flops 1207959552 | bytes 2490368 | tf_op jit(solution)/shard_map/dot_general | solution.py:81
  99.7 0.7 slice.15
  100.4 3.4 %all-to-all-start.1 = ((bf16[8,16,1024]{2,1,0:T(8,128)(2,1)}), bf16[8,16,1024]{2,1,0:T(8,128)(2,1)S(1)}, u32[]{:S(2)}, u32[]{:S(2)}) async-start(bf16[8,16,1024]{2,1,0:T(8,128)(2,1)} %bitcast.6), calls=%async_computation.2 | async-start | bytes 524288 | tf_op jit(solution)/shard_map/all_to_all | solution.py:88
  103.8 1.1 fusion
  104.9 5.7 %all-to-all-done.1 = bf16[8,16,1024]{2,1,0:T(8,128)(2,1)S(1)} async-done(((bf16[8,16,1024]{2,1,0:T(8,128)(2,1)}), bf16[8,16,1024]{2,1,0:T(8,128)(2,1)S(1)}, u32[]{:S(2)}, u32[]{:S(2)}) %all-to-all-start.1) | async-done | bytes 262176 | tf_op jit(solution)/shard_map/all_to_all | solution.py:88
  110.7 28.1 %all-reduce.2.cloned.1.call-done = f32[128,1024]{1,0:T(8,128)} async-done(((f32[128,1024]{1,0:T(8,128)}), f32[128,1024]{1,0:T(8,128)}) %all-reduce.2.cloned.1.call-update) | async-done | bytes 524304 | tf_op jit(solution)/shard_map/psum | solution.py:80
  138.8 1.9 %copy.38 = f32[128,1024]{1,0:T(8,128)} copy(f32[128,1024]{1,0:T(8,128)} %all-reduce.2.cloned.1.call-done) | data formatting | bytes 1048576
  140.7 0.7 copy.39
  141.4 0.7 copy.40
  (12 shorter events, 0.1 us)
Async XLA Ops:
  7.2 96.7 %copy-start = (bf16[128,1024]{1,0:T(8,128)(2,1)S(1)}, bf16[128,1024]{1,0:T(8,128)(2,1)}, u32[]{:S(2)}) copy-start(bf16[128,1024]{1,0:T(8,128)(2,1)} %param.22) | copy-start | bytes 786436
  7.2 33.2 %all-gather.2.cloned.1.call-start = ((), (), s32[]{:S(2)}) async-start(), calls=%async_computation.3 | async-start | bytes 2359296 | tf_op jit(solution)/shard_map/all_gather | solution.py:63
  7.9 89.9 %reduce-scatter.2.cloned.1.call-start = ((), (), s32[]{:S(2)}) async-start(), calls=%async_computation.4 | async-start | bytes 4718592 | tf_op jit(solution)/shard_map/reduce_scatter | solution.py:79
  14.6 29.0 %copy-start.1 = (bf16[256,1024]{1,0:T(8,128)(2,1)S(1)}, bf16[256,1024]{1,0:T(8,128)(2,1)}, u32[]{:S(2)}) copy-start(bf16[256,1024]{1,0:T(8,128)(2,1)} %param.21) | copy-start | bytes 1572868
  46.5 0.7 copy-start.3
  46.5 1.0 copy-start.2
  49.1 10.3 %all-to-all-start = ((bf16[8,16,1024]{2,1,0:T(8,128)(2,1)}), bf16[8,16,1024]{2,1,0:T(8,128)(2,1)S(1)}, u32[]{:S(2)}, u32[]{:S(2)}) async-start(bf16[8,16,1024]{2,1,0:T(8,128)(2,1)} %broadcast_select_fusion), calls=%async_computation.1 | async-start | bytes 524288 | tf_op jit(solution)/shard_map/all_to_all | solution.py:47
  52.5 86.3 %all-reduce.2.cloned.1.call-start = ((), (), s32[]{:S(2)}) async-start(), calls=%async_computation.5 | async-start | bytes 1048576 | tf_op jit(solution)/shard_map/psum | solution.py:80
  100.4 10.3 %all-to-all-start.1 = ((bf16[8,16,1024]{2,1,0:T(8,128)(2,1)}), bf16[8,16,1024]{2,1,0:T(8,128)(2,1)S(1)}, u32[]{:S(2)}, u32[]{:S(2)}) async-start(bf16[8,16,1024]{2,1,0:T(8,128)(2,1)} %bitcast.6), calls=%async_computation.2 | async-start | bytes 524288 | tf_op jit(solution)/shard_map/all_to_all | solution.py:88
Sparse Core Ops, SparseCore 0:
  9.9 30.4 all-gather.1
  46.6 51.1 reduce-scatter.1
  100.1 38.6 all-reduce.1
where the time goes:
time: 149 us
  waiting for transfers between devices  102 us (68%)
  matrix products  15.3 us (10%)
  between operations  13.8 us (9%)
  starting transfers between devices  6.95 us (5%)
  local copies, waits for them, and re-layouts  5.91 us (4%)
  other arithmetic  4.51 us (3%)
    reduce_scatter x1, waiting for transfers between devices, local(): lax.psum_scatter(partial_value, 'dom', scatter_dimension=0, tiled=True)  35 us
    psum x1, waiting for transfers between devices, local(): weight_grad = lax.psum(block_sum, 'group')  28.1 us
    all_gather x1, waiting for transfers between devices, local(): lax.all_gather(weight, 'dom', axis=0, tiled=True)  25.8 us
    all_to_all x1, waiting for transfers between devices, local(): lax.all_to_all(outgoing, 'dom', split_axis=0, concat_axis=0, tiled=True)  6.71 us
    all_to_all x1, waiting for transfers between devices, local(): lax.all_to_all(bound_grad, 'dom', split_axis=0, concat_axis=0, tiled=True)  5.75 us
    unnamed x11, local copies, waits for them, and re-layouts  4.15 us
    all_to_all x1, starting transfers between devices, local(): lax.all_to_all(outgoing, 'dom', split_axis=0, concat_axis=0, tiled=True)  3.42 us
    all_to_all x1, starting transfers between devices, local(): lax.all_to_all(bound_grad, 'dom', split_axis=0, concat_axis=0, tiled=True)  3.41 us
  transfers between devices with their start and end apart: 5, of which 5 were waited for; matrix products, arithmetic and copies ran while one was open for 10% of the time, Pallas kernels for 0%

commit v1 on v0

--- a/solution.py
+++ b/solution.py
@@ -77,7 +77,8 @@
         hidden, pre_grad, (((0,), (0,)), ((), ())), preferred_element_type=jnp.float32
     )
     block_sum = lax.psum_scatter(partial_value, "dom", scatter_dimension=0, tiled=True)
-    weight_grad = lax.psum(block_sum, "group")
+    shards = lax.all_gather(block_sum, "group", axis=0, tiled=False)
+    weight_grad = shards.sum(axis=0)
     src_grad = lax.dot_general(
         operator,
         hid_grad.astype(jnp.float32),

time: 149 us -> 156 us (1.047)
  waiting for transfers between devices: 102 us -> 111 us
  local copies, waits for them, and re-layouts: 5.91 us -> 3.19 us
  other arithmetic: 4.51 us -> 7.11 us
  matrix products: 15.3 us -> 13.4 us
    psum x1 -> x0, waiting for transfers between devices: 28.1 us -> none  [local(): weight_grad = lax.psum(block_sum, 'group')]
    all_gather x0 -> x1, waiting for transfers between devices: none -> 20.8 us  [local(): shards = lax.all_gather(block_sum, 'group', axis=0, tiled=False)]
    reduce_scatter x1, waiting for transfers between devices: 35 us -> 51.2 us  [local(): lax.psum_scatter(partial_value, 'dom', scatter_dimension=0, tiled=True)]
    unnamed x11 -> x10, local copies, waits for them, and re-layouts: 4.15 us -> 1.43 us
    reduce_sum x0 -> x1, other arithmetic: none -> 2.59 us  [local(): weight_grad = shards.sum(axis=0)]
  transfers between devices with their start and end apart: 5 -> 5, of which waited for: 5 -> 5; matrix products, arithmetic and copies ran while one was open for 10% -> 9% of each run, Pallas kernels for 0% -> 0%
where the time goes in v1:
time: 156 us
  waiting for transfers between devices  111 us (71%)
  between operations  13.9 us (9%)
  matrix products  13.4 us (9%)
  other arithmetic  7.11 us (5%)
  starting transfers between devices  6.94 us (4%)
  local copies, waits for them, and re-layouts  3.19 us (2%)
    reduce_scatter x1, waiting for transfers between devices, local(): lax.psum_scatter(partial_value, 'dom', scatter_dimension=0, tiled=True)  51.2 us
    all_gather x1, waiting for transfers between devices, local(): lax.all_gather(weight, 'dom', axis=0, tiled=True)  25.8 us
    all_gather x1, waiting for transfers between devices, local(): shards = lax.all_gather(block_sum, 'group', axis=0, tiled=False)  20.8 us
    all_to_all x1, waiting for transfers between devices, local(): lax.all_to_all(outgoing, 'dom', split_axis=0, concat_axis=0, tiled=True)  6.76 us
    all_to_all x1, waiting for transfers between devices, local(): lax.all_to_all(bound_grad, 'dom', split_axis=0, concat_axis=0, tiled=True)  5.74 us
    all_to_all x1, starting transfers between devices, local(): lax.all_to_all(bound_grad, 'dom', split_axis=0, concat_axis=0, tiled=True)  3.41 us
    all_to_all x1, starting transfers between devices, local(): lax.all_to_all(outgoing, 'dom', split_axis=0, concat_axis=0, tiled=True)  3.41 us
    dot_general x1, matrix products, local(): jnp.dot(hidden, lax.all_gather(weight, 'dom', axis=0, tiled=True), prefer...  3.18 us
  transfers between devices with their start and end apart: 5, of which 5 were waited for; matrix products, arithmetic and copies ran while one was open for 9% of the time, Pallas kernels for 0%

profile of v1, /device:TPU:0, one launch (start us, length us, event | category | flops | bytes accessed | tf_op | source)
XLA Modules:
  0.0 155.6 jit_solution(9613588030354754084)
XLA Ops:
  7.2 0.0 all-gather.4.cloned.1.call-start
  7.2 0.7 all-gather.4.cloned.1.call-update
  7.9 0.0 reduce-scatter.2.cloned.1.call-start
  8.0 0.9 select_reduce_fusion
  8.8 0.7 iota_compare_fusion.4
  9.6 1.0 broadcast_select_fusion.1
  10.6 1.1 multiply_convert_fusion.2
  11.6 1.0 fusion.11
  12.6 2.0 %convolution_convert_fusion = bf16[256,1024]{1,0:T(8,128)(2,1)S(1)} fusion(bf16[128,1024]{1,0:T(8,128)(2,1)} %param.16, bf16[128,1024]{1,0:T(8,128)(2,1)S(1)} %multiply_convert_fusion.2, bf16[128,1024]{1,0:T(8,128)(2,1)} %param.12, f32[32,8,3,128]{3,2,1,0:T(4,128)S(1)} %bitcast.27), kind=kOutput, calls=%fused_computation.2 | convolution fusion | flops 1210580992 | bytes 1703936 | tf_op jit(solution)/shard_map/dot_general | solution.py:59
  14.6 25.8 %all-gather.4.cloned.1.call-done = bf16[1024,1024]{1,0:T(8,128)(2,1)} async-done(((bf16[128,1024]{1,0:T(8,128)(2,1)}), bf16[1024,1024]{1,0:T(8,128)(2,1)}) %all-gather.4.cloned.1.call-update) | async-done | bytes 2097168 | tf_op jit(solution)/shard_map/all_gather | solution.py:63
  40.4 3.2 %multiply_convert_fusion.1 = (bf16[256,1024]{1,0:T(8,128)(2,1)}, f32[256,1024]{1,0:T(8,128)S(1)}) fusion(bf16[256,1024]{1,0:T(8,128)(2,1)S(1)} %convolution_convert_fusion, bf16[1024,1024]{1,0:T(8,128)(2,1)} %all-gather.4.cloned.1.call-done), kind=kOutput, calls=%fused_computation.6 | convolution fusion | flops 538181632 | bytes 4194304 | tf_op jit(solution)/shard_map/dot_general | solution.py:61
  43.6 2.9 %fusion.19 = f32[1024,1024]{1,0:T(8,128)} fusion(bf16[256,1024]{1,0:T(8,128)(2,1)S(1)} %convolution_convert_fusion, f32[256,1024]{1,0:T(8,128)S(1)} %get-tuple-element.6, bf16[256,1024]{1,0:T(8,128)(2,1)S(1)} %copy-done.1), kind=kOutput, calls=%fused_computation.39 | convolution fusion | flops 539492352 | bytes 6291456 | tf_op jit(solution)/shard_map/dot_general | solution.py:76
  46.5 0.0 reduce-scatter.2.cloned.1.call-update
  46.5 0.0 all-gather.6.cloned.1.call-start
  46.5 51.2 %reduce-scatter.2.cloned.1.call-done = f32[128,1024]{1,0:T(8,128)} async-done(((f32[1024,1024]{1,0:T(8,128)}), f32[128,1024]{1,0:T(8,128)}) %reduce-scatter.2.cloned.1.call-update) | async-done | bytes 524304 | tf_op jit(solution)/shard_map/reduce_scatter | solution.py:79
  97.8 0.0 all-gather.6.cloned.1.call-update
  97.8 0.1 reshape.86
  98.0 0.9 gather_fusion
  98.8 0.8 broadcast_select_fusion
  99.6 3.4 %all-to-all-start = ((bf16[8,16,1024]{2,1,0:T(8,128)(2,1)}), bf16[8,16,1024]{2,1,0:T(8,128)(2,1)S(1)}, u32[]{:S(2)}, u32[]{:S(2)}) async-start(bf16[8,16,1024]{2,1,0:T(8,128)(2,1)} %broadcast_select_fusion), calls=%async_computation.1 | async-start | bytes 524288 | tf_op jit(solution)/shard_map/all_to_all | solution.py:47
  103.1 0.1 eq.48
  103.1 6.8 %all-to-all-done = bf16[8,16,1024]{2,1,0:T(8,128)(2,1)S(1)} async-done(((bf16[8,16,1024]{2,1,0:T(8,128)(2,1)}), bf16[8,16,1024]{2,1,0:T(8,128)(2,1)S(1)}, u32[]{:S(2)}, u32[]{:S(2)}) %all-to-all-start) | async-done | bytes 262176 | tf_op jit(solution)/shard_map/all_to_all | solution.py:47
  109.9 2.5 %convolution_convert_fusion.1 = bf16[256,1024]{1,0:T(8,128)(2,1)S(1)} fusion(bf16[1024,1024]{1,0:T(8,128)(2,1)} %all-gather.4.cloned.1.call-done, f32[256,1024]{1,0:T(8,128)S(1)} %get-tuple-element.6, bf16[256,1024]{1,0:T(8,128)(2,1)S(1)} %copy-done.1), kind=kOutput, calls=%fused_computation.4 | convolution fusion | flops 539754496 | bytes 4194304 | tf_op jit(solution)/shard_map/dot_general | solution.py:69
  112.4 0.8 fusion.7
  113.2 0.7 slice.15
  113.9 3.4 %all-to-all-start.1 = ((bf16[8,16,1024]{2,1,0:T(8,128)(2,1)}), bf16[8,16,1024]{2,1,0:T(8,128)(2,1)S(1)}, u32[]{:S(2)}, u32[]{:S(2)}) async-start(bf16[8,16,1024]{2,1,0:T(8,128)(2,1)} %bitcast.7), calls=%async_computation.2 | async-start | bytes 524288 | tf_op jit(solution)/shard_map/all_to_all | solution.py:89
  117.4 1.1 fusion
  118.5 5.7 %all-to-all-done.1 = bf16[8,16,1024]{2,1,0:T(8,128)(2,1)S(1)} async-done(((bf16[8,16,1024]{2,1,0:T(8,128)(2,1)}), bf16[8,16,1024]{2,1,0:T(8,128)(2,1)S(1)}, u32[]{:S(2)}, u32[]{:S(2)}) %all-to-all-start.1) | async-done | bytes 262176 | tf_op jit(solution)/shard_map/all_to_all | solution.py:89
  124.2 20.8 %all-gather.6.cloned.1.call-done = f32[512,1024]{1,0:T(8,128)} async-done(((f32[128,1024]{1,0:T(8,128)}), f32[512,1024]{1,0:T(8,128)}) %all-gather.6.cloned.1.call-update) | async-done | bytes 2097168 | tf_op jit(solution)/shard_map/all_gather | solution.py:80
  145.0 2.6 %reduce_sum.19 = f32[128,1024]{1,0:T(8,128)} reduce(f32[4,128,1024]{2,1,0:T(8,128)} %bitcast.26, f32[]{:T(128)} %constant.8.clone.1), dimensions={0}, to_apply=%region_2.3 | reduce | flops 393216 | bytes 2621444 | tf_op jit(solution)/shard_map/reduce_sum | solution.py:81
  147.6 0.7 copy.37
  148.3 0.7 copy.38
  (12 shorter events, 0.1 us)
Async XLA Ops:
  7.2 110.2 %copy-start = (bf16[128,1024]{1,0:T(8,128)(2,1)S(1)}, bf16[128,1024]{1,0:T(8,128)(2,1)}, u32[]{:S(2)}) copy-start(bf16[128,1024]{1,0:T(8,128)(2,1)} %param.22) | copy-start | bytes 786436
  7.2 33.2 %all-gather.4.cloned.1.call-start = ((), (), s32[]{:S(2)}) async-start(), calls=%async_computation.3 | async-start | bytes 2359296 | tf_op jit(solution)/shard_map/all_gather | solution.py:63
  7.9 89.9 %reduce-scatter.2.cloned.1.call-start = ((), (), s32[]{:S(2)}) async-start(), calls=%async_computation.4 | async-start | bytes 4718592 | tf_op jit(solution)/shard_map/reduce_scatter | solution.py:79
  14.6 29.0 %copy-start.1 = (bf16[256,1024]{1,0:T(8,128)(2,1)S(1)}, bf16[256,1024]{1,0:T(8,128)(2,1)}, u32[]{:S(2)}) copy-start(bf16[256,1024]{1,0:T(8,128)(2,1)} %param.21) | copy-start | bytes 1572868
  46.5 51.3 %copy-start.3 = (s32[8,16]{1,0:T(8,128)S(1)}, s32[8,16]{1,0:T(8,128)}, u32[]{:S(2)}) copy-start(s32[8,16]{1,0:T(8,128)} %param.23) | copy-start | bytes 1540
  46.5 51.5 %copy-start.2 = (bf16[128,1024]{1,0:T(8,128)(2,1)S(1)}, bf16[128,1024]{1,0:T(8,128)(2,1)}, u32[]{:S(2)}) copy-start(bf16[128,1024]{1,0:T(8,128)(2,1)} %param.12) | copy-start | bytes 786436
  46.5 98.6 %all-gather.6.cloned.1.call-start = ((), (), s32[]{:S(2)}) async-start(), calls=%async_computation.5 | async-start | bytes 2621440 | tf_op jit(solution)/shard_map/all_gather | solution.py:80
  99.6 10.3 %all-to-all-start = ((bf16[8,16,1024]{2,1,0:T(8,128)(2,1)}), bf16[8,16,1024]{2,1,0:T(8,128)(2,1)S(1)}, u32[]{:S(2)}, u32[]{:S(2)}) async-start(bf16[8,16,1024]{2,1,0:T(8,128)(2,1)} %broadcast_select_fusion), calls=%async_computation.1 | async-start | bytes 524288 | tf_op jit(solution)/shard_map/all_to_all | solution.py:47
  113.9 10.3 %all-to-all-start.1 = ((bf16[8,16,1024]{2,1,0:T(8,128)(2,1)}), bf16[8,16,1024]{2,1,0:T(8,128)(2,1)S(1)}, u32[]{:S(2)}, u32[]{:S(2)}) async-start(bf16[8,16,1024]{2,1,0:T(8,128)(2,1)} %bitcast.7), calls=%async_computation.2 | async-start | bytes 524288 | tf_op jit(solution)/shard_map/all_to_all | solution.py:89
Sparse Core Ops, SparseCore 0:
  9.9 30.4 all-gather.3
  46.6 51.1 reduce-scatter.1
  99.4 45.6 all-gather.5
